TPU v7x, 256 devices: a whole 4x4x8 slice. The times are simulated.
256 devices in a mesh: chan: 32 (over x_lo, z, core), stn: 8 (over x_hi, y).
Axes of the slice: x: 4 (x_hi: 2, x_lo: 2; x = x_hi * 2 + x_lo), y: 4, z: 8, core: 2. Of those that a mesh axis runs over, the one named last changes fastest.
Arguments:
- voltages: bfloat16 [32, 2, 1024, 512], P(None, None, ('stn', 'chan')), may hold values from -6 to 6
- phase_index: int32 [1024], P(('stn', 'chan')), may hold values from 0 to 1023
- int_lengths: int32 [4], replicated, may hold values from 1 to 192, 512 in all
- beam_weights: bfloat16 [2, 256, 1024], replicated, may hold values from -0.1875 to 0.1875
Outputs:
- visibilities: bfloat16 [8, 5, 4, 32, 2, 128, 128], P('stn', None, None, 'chan')
- beam_power: float32 [4, 32, 256], P(None, 'chan', 'stn')
Inputs may be any that keep to these rules, and one draw needn't show every extreme that they name: `int_lengths`: 4 integration lengths summing to 512; the longest is exactly 192.
All inputs are finite; a program needn't handle non-finite values.
Results may differ from a plain program's by a relative error of at most 0.0055.
Values may be sent and summed in bfloat16 or wider, within the bound.
A program may use at most 64 MiB of HBM per device.

v0:
```python
import math
import jax
import jax.numpy as jnp
from jax import lax
from jax.sharding import PartitionSpec as P

INTEG = 4
MOST = 192
BEAMS = 256
PHASES = 1024
full_turn = 2.0 * math.pi


def rotate(voltages, phase_index, channel):
    phase_turns = channel[:, None] * phase_index[None, :] % PHASES
    phase_angle = phase_turns.astype(jnp.float32) * (full_turn / PHASES)
    cosine = jnp.cos(phase_angle)[:, :, None]
    sine_part = jnp.sin(phase_angle)[:, :, None]
    real_in = voltages[:, 0].astype(jnp.float32)
    imag_in = voltages[:, 1].astype(jnp.float32)
    return jnp.stack(
        [real_in * cosine + imag_in * sine_part, imag_in * cosine - real_in * sine_part], axis=1
    ).astype(jnp.bfloat16)


def windows(block, starts, int_lengths):
    padded = jnp.pad(block, ((0, 0), (0, 0), (0, MOST)))
    in_range = jnp.arange(MOST, dtype=jnp.int32)
    result = []
    for period in range(INTEG):
        segment = lax.dynamic_slice_in_dim(padded, starts[period], MOST, 2)
        keep_mask = (in_range < int_lengths[period])[None, None, :]
        result.append(jnp.where(keep_mask, segment, jnp.zeros_like(segment)))
    return jnp.stack(result)


def correlate(own_parts, other, starts, int_lengths):
    padded = jnp.pad(other, ((0, 0), (0, 0), (0, MOST)))
    block_rows = own_parts.shape[2] // 2
    result = []
    for period in range(INTEG):
        segment = lax.dynamic_slice_in_dim(padded, starts[period], MOST, 2)
        products = jnp.einsum(
            "cal,cbl->cab", own_parts[period], segment, preferred_element_type=jnp.float32
        )
        real_part = products[:, :block_rows, :block_rows] + products[:, block_rows:, block_rows:]
        imag_part = products[:, block_rows:, :block_rows] - products[:, :block_rows, block_rows:]
        inverse = 1.0 / int_lengths[period].astype(jnp.float32)
        result.append((jnp.stack([real_part, imag_part], axis=1) * inverse).astype(jnp.bfloat16))
    return jnp.stack(result)


def stack_weights(beam_weights, beam_first, beam_count, column_first, column_count):
    weight_real = lax.dynamic_slice(
        beam_weights[0], (beam_first, column_first), (beam_count, column_count)
    )
    weight_imag = lax.dynamic_slice(
        beam_weights[1], (beam_first, column_first), (beam_count, column_count)
    )
    upper = jnp.concatenate([weight_real, -weight_imag], axis=1)
    lower = jnp.concatenate([weight_imag, weight_real], axis=1)
    return jnp.concatenate([upper, lower], axis=0)


def integrate(power, starts, int_lengths, form):
    samples = power.shape[-1]
    sample_index = jnp.arange(samples, dtype=jnp.int32)[None, :]
    in_window = (
        (sample_index >= starts[:, None]) & (sample_index < (starts + int_lengths)[:, None])
    ).astype(jnp.float32)
    summed = jnp.einsum(form, power, in_window, precision=lax.Precision.HIGHEST)
    return summed / int_lengths.astype(jnp.float32)[:, None, None]


def local(voltages, phase_index, int_lengths, beam_weights):
    channel = jnp.arange(voltages.shape[0], dtype=jnp.int32)
    rotated = rotate(voltages, phase_index, channel)
    turned = lax.all_to_all(rotated, "chan", split_axis=0, concat_axis=2, tiled=True)
    station = lax.axis_index("stn")
    stations = lax.axis_size("stn")
    halfway = stations // 2
    share = BEAMS // stations
    ch_local, _, block_rows, samples = turned.shape
    own = turned.reshape(ch_local, 2 * block_rows, samples)
    starts = jnp.cumsum(int_lengths) - int_lengths
    own_parts = windows(own, starts, int_lengths)

    def place(vis_total, other, offset):
        fresh = correlate(own_parts, other, starts, int_lengths)
        return lax.dynamic_update_slice(vis_total, fresh[None], (offset, 0, 0, 0, 0, 0))

    def leave(vis_total, other, offset):
        return vis_total

    vis_start = jnp.zeros((halfway + 1, INTEG, ch_local, 2, block_rows, block_rows), jnp.bfloat16)
    beam_start = jnp.zeros((ch_local, 2 * share, samples), jnp.float32)
    portion = lax.all_gather(turned, "stn", axis=2, tiled=True)
    first_row = jnp.int32(0)
    vis_total = vis_start
    beam_total = beam_start
    for member in range(portion.shape[2] // block_rows):
        other = portion[:, :, member * block_rows : (member + 1) * block_rows, :].reshape(
            ch_local, 2 * block_rows, samples
        )
        other_index = first_row // block_rows + member
        offset = (other_index - station) % stations
        vis_total = lax.cond(offset <= halfway, place, leave, vis_total, other, offset)
        stacked = stack_weights(
            beam_weights, station * share, share, other_index * block_rows, block_rows
        )
        partial_beam = jnp.einsum("rk,ckt->crt", stacked, other, preferred_element_type=jnp.float32)
        beam_total = beam_total + lax.optimization_barrier(
            partial_beam.astype(jnp.bfloat16)
        ).astype(jnp.float32)
    vis_total, beam_total = (vis_total, beam_total)
    beam_total = beam_total.reshape(ch_local, 2, share, samples)
    power = beam_total[:, 0] ** 2 + beam_total[:, 1] ** 2
    beam_power = integrate(power, starts, int_lengths, "cbt,jt->jcb")
    return (vis_total[None], beam_power)


def solution(mesh):
    return jax.shard_map(
        local,
        mesh=mesh,
        in_specs=(P(None, None, ("stn", "chan"), None), P(("stn", "chan")), P(), P()),
        out_specs=(P("stn", None, None, "chan", None, None, None), P(None, "chan", "stn")),
        check_vma=False,
    )
```

profile of v0, /device:TPU:1, one launch (start us, length us, event | category | flops | bytes accessed | tf_op | source)
XLA Modules:
  0.0 167.8 jit_solution(5252909715909642435)
XLA Ops:
  7.2 0.8 fusion.347
  8.0 0.1 copy.12
  8.1 0.1 copy.13
  8.2 1.2 fusion.273
  9.4 0.2 pad_maximum_fusion
  9.6 22.5 %all_to_all.18 = bf16[32,2,4,512]{3,2,1,0:T(4,128)(2,1)S(1)} all-to-all(bf16[32,2,4,512]{3,2,1,0:T(4,128)(2,1)S(1)} %pad_maximum_fusion), channel_id=1, replica_groups=mesh['chan'=32,'stn'=8] {'chan'}, dimensions={0} | all-to-all | bytes 524288 | tf_op jit(solution)/shard_map/all_to_all | solution.py:78
  32.1 0.1 copy.14
  32.2 0.8 all_to_all.16
  33.0 0.2 reduce-window.8
  33.2 0.6 fusion.384
  40.9 0.6 fusion.383
  41.5 1.2 iota_compare_fusion.3
  42.7 1.1 iota_compare_fusion.5
  44.0 0.3 fusion.279
  44.3 44.1 %all-gather.2.cloned.1.call-done = bf16[1,2,1024,512]{3,2,1,0:T(8,128)(2,1)} async-done(((bf16[1,2,128,512]{3,2,1,0:T(8,128)(2,1)}), bf16[1,2,1024,512]{3,2,1,0:T(8,128)(2,1)}) %all-gather.2.cloned.1.call-update) | async-done | bytes 2097168 | tf_op jit(solution)/shard_map/all_gather | solution.py:97
  88.4 1.7 %fusion.380 = (bf16[1,2,128,512]{3,2,1,0:T(8,128)(2,1)S(1)}, bf16[1,2,128,512]{3,2,1,0:T(8,128)(2,1)S(1)}, bf16[1,2,128,512]{3,2,1,0:T(8,128)(2,1)S(1)}, bf16[1,...) fusion(bf16[1,2,1024,512]{3,2,1,0:T(8,128)(2,1)} %all-gather.2., ...), kind=kLoop, calls=%fused_computation.561 | loop fusion | bytes 4194304 | tf_op jit(solution)/shard_map/slice | solution.py:102
  90.1 0.2 fusion.264
  90.3 0.2 fusion.265
  90.4 0.2 fusion.266
  90.6 0.2 fusion.267
  90.8 0.2 fusion.268
  90.9 0.2 fusion.269
  91.1 0.2 fusion.270
  91.3 0.2 fusion.271
  91.4 13.8 %conditional.8 = (bf16[5,4,1,2,128,128]{4,5,3,1,2,0:T(8,128)(2,1)}) conditional(s32[]{:T(128)} %convert_element_type.674, () %tuple.58, (bf16[1,2,128,512]{3,2,1,0:T(8,128)(2,1)S(1)}, s32[4]{0:T(128)S(1)}, bf16[1,256,192]{2,1,0:T(8,128)(2,1)S(1)}, s32[4]{0:T(128)S(1)}, bf16[1,256,192]{2,1,0:T(8,128)(2,1)S(1)}, ...), branch_computations={%region_1.2_spmd, %region_2.3_spmd} | conditional | flops 102236168 | bytes 6685032 | solution.py:107
  91.5 0.7 fusion.364
  93.8 0.2 convolution_bitcast_fusion.2
  96.6 0.2 convolution_bitcast_fusion.1
  99.3 0.2 convolution_bitcast_fusion
  102.2 0.2 convolution_bitcast_fusion.3
  103.1 1.4 broadcast_in_dim.57
  104.5 0.7 fusion
  105.2 13.0 %conditional.9 = (bf16[5,4,1,2,128,128]{4,5,3,1,2,0:T(8,128)(2,1)}) conditional(s32[]{:T(128)} %convert_element_type.673, bf16[5,4,1,2,128,128]{4,5,3,1,2,0:T(8,128)(2,1)} %get-tuple-element.511, (bf16[1,2,128,512]{3,2,1,0:T(8,128)(2,1)S(1)}, s32[4]{0:T(128)S(1)}, bf16[1,256,192]{2,1,0:T(8,128)(2,1)S(1)}, s32[4]{0:T(128)S(1)}, ...), branch_computations={%region_3.4_spmd, %region_4.5_spmd} | conditional | flops 102236168 | bytes 5374310 | solution.py:107
  105.2 0.7 fusion.366
  108.0 0.2 convolution_bitcast_fusion.7
  110.9 0.2 convolution_bitcast_fusion.6
  113.7 0.2 convolution_bitcast_fusion.5
  116.5 0.2 convolution_bitcast_fusion.4
  117.5 0.7 fusion.33
  118.2 13.0 %conditional.10 = (bf16[5,4,1,2,128,128]{4,5,3,1,2,0:T(8,128)(2,1)}) conditional(s32[]{:T(128)} %convert_element_type.672, bf16[5,4,1,2,128,128]{4,5,3,1,2,0:T(8,128)(2,1)} %get-tuple-element.512, (bf16[1,2,128,512]{3,2,1,0:T(8,128)(2,1)S(1)}, s32[4]{0:T(128)S(1)}, bf16[1,256,192]{2,1,0:T(8,128)(2,1)S(1)}, s32[4]{0:T(128)S(1)}, ...), branch_computations={%region_5.6_spmd, %region_6.7_spmd} | conditional | flops 102236168 | bytes 5374310 | solution.py:107
  118.2 0.7 fusion.368
  121.0 0.2 convolution_bitcast_fusion.11
  124.0 0.2 convolution_bitcast_fusion.10
  126.8 0.2 convolution_bitcast_fusion.9
  129.6 0.2 convolution_bitcast_fusion.8
  130.5 0.7 fusion.66
  131.2 13.0 %conditional.11 = (bf16[5,4,1,2,128,128]{4,5,3,1,2,0:T(8,128)(2,1)}) conditional(s32[]{:T(128)} %convert_element_type.671, bf16[5,4,1,2,128,128]{4,5,3,1,2,0:T(8,128)(2,1)} %get-tuple-element.513, (bf16[1,2,128,512]{3,2,1,0:T(8,128)(2,1)S(1)}, s32[4]{0:T(128)S(1)}, bf16[1,256,192]{2,1,0:T(8,128)(2,1)S(1)}, s32[4]{0:T(128)S(1)}, ...), branch_computations={%region_7.8_spmd, %region_8.9_spmd} | conditional | flops 102236168 | bytes 5374310 | solution.py:107
  131.2 0.7 fusion.370
  134.0 0.2 convolution_bitcast_fusion.15
  137.0 0.2 convolution_bitcast_fusion.14
  139.8 0.2 convolution_bitcast_fusion.13
  142.6 0.2 convolution_bitcast_fusion.12
  143.5 0.7 fusion.99
  144.2 13.0 %conditional.12 = (bf16[5,4,1,2,128,128]{4,5,3,1,2,0:T(8,128)(2,1)}) conditional(s32[]{:T(128)} %convert_element_type.670, bf16[5,4,1,2,128,128]{4,5,3,1,2,0:T(8,128)(2,1)} %get-tuple-element.514, (bf16[1,2,128,512]{3,2,1,0:T(8,128)(2,1)S(1)}, s32[4]{0:T(128)S(1)}, bf16[1,256,192]{2,1,0:T(8,128)(2,1)S(1)}, s32[4]{0:T(128)S(1)}, ...), branch_computations={%region_9.10_spmd, %region_10.11_spmd} | conditional | flops 102236168 | bytes 5374310 | solution.py:107
  144.2 0.7 fusion.372
  147.0 0.2 convolution_bitcast_fusion.19
  150.0 0.2 convolution_bitcast_fusion.18
  152.8 0.2 convolution_bitcast_fusion.17
  155.6 0.2 convolution_bitcast_fusion.16
  156.5 0.7 fusion.132
  157.3 0.8 convolution_divide_fusion
  158.1 1.8 %conditional.15 = (bf16[1,5,4,1,2,128,128]{6,5,4,3,2,1,0:T(8,128)(2,1)S(1)}) conditional(s32[]{:T(128)} %convert_element_type.667, bf16[5,4,1,2,128,128]{4,5,3,1,0,2:T(8,128)(2,1)} %bitcast.320, (bf16[5,4,1,2,128,128]{4,5,3,1,2,0:T(8,128)(2,1)}, bf16[1,2,128,512]{3,2,1,0:T(8,128)(2,1)S(1)}, s32[4]{0:T(128)S(1)}, ...), branch_computations={%region_15.16_spmd, %region_16.17_spmd} | conditional | flops 102236168 | bytes 7995750 | solution.py:107
  158.1 1.8 %copy.20 = bf16[1,5,4,1,2,128,128]{6,5,4,3,2,1,0:T(8,128)(2,1)S(1)} copy(bf16[1,5,4,1,2,128,128]{5,6,4,2,3,1,0:T(8,128)(2,1)} %bitcast.266) | data formatting | bytes 2621440 | tf_op jit(solution)/shard_map/cond
  159.9 1.0 copy-done
  (55 shorter events, 1.0 us)
Async XLA Ops:
  7.2 81.2 %all-gather.2.cloned.1.call-start = ((), (), s32[]{:S(2)}) async-start(), calls=%async_computation.1 | async-start | bytes 2359296 | tf_op jit(solution)/shard_map/all_gather | solution.py:97
  9.4 23.6 %copy-start.2 = (s32[4]{0:T(128)S(1)}, s32[4]{0:T(128)}, u32[]{:S(2)}) copy-start(s32[4]{0:T(128)} %param.22) | copy-start | bytes 52
  9.4 34.4 %copy-start.1 = (bf16[2,256,1024]{2,1,0:T(8,128)(2,1)S(1)}, bf16[2,256,1024]{2,1,0:T(8,128)(2,1)}, u32[]{:S(2)}) copy-start(bf16[2,256,1024]{2,1,0:T(8,128)(2,1)} %param.23) | copy-start | bytes 3145732
  159.9 1.1 copy-start
Sparse Core Ops, SparseCore 0:
  33.1 55.2 all-gather.1
where the time goes:
time: 169 us; the launch traced here: 168 us
  loops' own time  52 us (31%)
  waiting for transfers between devices  44.1 us (26%)
  blocking collectives  22.5 us (13%)
  between operations  21.3 us (13%)
  local copies, waits for them, and re-layouts  11.7 us (7%)
  other arithmetic  9.31 us (6%)
  matrix products  6.89 us (4%)
    another operation x8, loops' own time, local(): lax.cond(offset <= halfway, place, leave, vis_total, other, offset)  52 us
    all_gather x1, waiting for transfers between devices, local(): portion = lax.all_gather(turned, 'stn', axis=2, tiled=True)  44.1 us
    all_to_all x1, blocking collectives, local(): lax.all_to_all(rotated, 'chan', split_axis=0, concat_axis=2, tiled=True)  22.5 us
    dot_general x20, matrix products, correlate(): jnp.einsum('cal,cbl->cab', own_parts[period], segment, preferred_element_...  4.83 us
    dynamic_update_slice x5, other arithmetic, place(): lax.dynamic_update_slice(vis_total, fresh[None], (offset, 0, 0, 0, 0, 0))  3.64 us
    slice x5, local copies, waits for them, and re-layouts, correlate(): inverse = 1.0 / int_lengths[period].astype(jnp.float32)  3.38 us
  transfers between devices with their start and end apart: 1, of which 1 were waited for; matrix products, arithmetic and copies ran while one was open for 3% of the time, Pallas kernels for 0%

commit v1 on v0

--- a/solution.py
+++ b/solution.py
@@ -94,7 +94,12 @@
 
     vis_start = jnp.zeros((halfway + 1, INTEG, ch_local, 2, block_rows, block_rows), jnp.bfloat16)
     beam_start = jnp.zeros((ch_local, 2 * share, samples), jnp.float32)
-    portion = lax.all_gather(turned, "stn", axis=2, tiled=True)
+    portion = jnp.concatenate(
+        lax.all_to_all(
+            jnp.stack(lax.axis_size("stn") * [turned], axis=0), "stn", concat_axis=0, split_axis=0
+        ),
+        axis=2,
+    )
     first_row = jnp.int32(0)
     vis_total = vis_start
     beam_total = beam_start

time: 169 us -> 132 us (0.78)
  waiting for transfers between devices: 44.1 us -> 11.2 us
  between operations: 21.3 us -> 8.9 us
  starting transfers between devices: 0.04 us -> 6.49 us
  other arithmetic: 9.31 us -> 11.9 us
    all_gather x1 -> x0, waiting for transfers between devices: 44.1 us -> none  [local(): portion = lax.all_gather(turned, 'stn', axis=2, tiled=True)]
    all_to_all x0 -> x1, waiting for transfers between devices: none -> 11.2 us  [local(): lax.all_to_all(jnp.stack(lax.axis_size('stn') * [turned], axis=0), 'stn',...]
    all_to_all x0 -> x1, starting transfers between devices: none -> 6.49 us  [local(): lax.all_to_all(jnp.stack(lax.axis_size('stn') * [turned], axis=0), 'stn',...]
  transfers between devices with their start and end apart: 1 -> 1, of which waited for: 1 -> 1; matrix products, arithmetic and copies ran while one was open for 3% -> 5% of each run, Pallas kernels for 0% -> 0%
where the time goes in v1:
time: 132 us; the launch traced here: 131 us
  loops' own time  50.7 us (38%)
  blocking collectives  22.4 us (17%)
  local copies, waits for them, and re-layouts  12.5 us (9%)
  other arithmetic  11.9 us (9%)
  waiting for transfers between devices  11.2 us (8%)
  between operations  8.9 us (7%)
  matrix products  6.88 us (5%)
  starting transfers between devices  6.49 us (5%)
    another operation x8, loops' own time, local(): lax.cond(offset <= halfway, place, leave, vis_total, other, offset)  50.7 us
    all_to_all x1, blocking collectives, local(): lax.all_to_all(rotated, 'chan', split_axis=0, concat_axis=2, tiled=True)  22.4 us
    all_to_all x1, waiting for transfers between devices, local(): lax.all_to_all(jnp.stack(lax.axis_size('stn') * [turned], axis=0), 'stn',...  11.2 us
    all_to_all x1, starting transfers between devices, local(): lax.all_to_all(jnp.stack(lax.axis_size('stn') * [turned], axis=0), 'stn',...  6.49 us
    dot_general x20, matrix products, correlate(): jnp.einsum('cal,cbl->cab', own_parts[period], segment, preferred_element_...  4.83 us
    lt x2, other arithmetic, windows(): keep_mask = (in_range < int_lengths[period])[None, None, :]  3.72 us
    dynamic_update_slice x5, other arithmetic, place(): lax.dynamic_update_slice(vis_total, fresh[None], (offset, 0, 0, 0, 0, 0))  3.64 us
    slice x5, local copies, waits for them, and re-layouts, correlate(): inverse = 1.0 / int_lengths[period].astype(jnp.float32)  3.32 us
  transfers between devices with their start and end apart: 1, of which 1 were waited for; matrix products, arithmetic and copies ran while one was open for 5% of the time, Pallas kernels for 0%

profile of v1, /device:TPU:1, one launch (start us, length us, event | category | flops | bytes accessed | tf_op | source)
XLA Modules:
  0.0 130.9 jit_solution(6628900193765690310)
XLA Ops:
  0.6 0.8 fusion.347
  1.6 1.2 fusion.273
  2.8 0.2 pad_maximum_fusion
  3.0 22.4 %all_to_all.20 = bf16[32,2,4,512]{3,2,1,0:T(4,128)(2,1)S(1)} all-to-all(bf16[32,2,4,512]{3,2,1,0:T(4,128)(2,1)S(1)} %pad_maximum_fusion), channel_id=1, replica_groups=mesh['chan'=32,'stn'=8] {'chan'}, dimensions={0} | all-to-all | bytes 524288 | tf_op jit(solution)/shard_map/all_to_all | solution.py:78
  25.4 0.2 copy.35
  25.6 1.5 %stack.365 = bf16[8,1,2,128,512]{4,3,2,1,0:T(8,128)(2,1)} broadcast(bf16[2,128,512]{2,1,0:T(8,128)(2,1)S(1)} %copy.36), dimensions={2,3,4} | broadcast | bytes 2359296 | tf_op jit(solution)/shard_map/stack | solution.py:99
  27.1 6.5 %all-to-all-start.1 = ((bf16[8,1,2,128,512]{4,3,2,1,0:T(8,128)(2,1)}), bf16[8,1,2,128,512]{4,3,2,1,0:T(8,128)(2,1)S(1)}, u32[]{:S(2)}, u32[]{:S(2)}) async-start(bf16[8,1,2,128,512]{4,3,2,1,0:T(8,128)(2,1)} %stack.365), calls=%async_computation.1 | async-start | bytes 4194304 | tf_op jit(solution)/shard_map/all_to_all | solution.py:98
  33.6 0.2 reduce-window.8
  33.8 0.6 fusion.382
  34.4 0.7 fusion.384
  43.0 0.7 fusion.383
  43.7 1.8 %iota_compare_fusion.3 = (pred[192]{0:T(512)(128)(4,1)}, pred[192]{0:T(512)(128)(4,1)}) fusion(s32[]{:T(128)} %bitcast.321, s32[]{:T(128)} %bitcast.319), kind=kLoop, calls=%fused_computation.522 | loop fusion | flops 384 | bytes 392 | tf_op jit(solution)/shard_map/lt | solution.py:32
  45.5 1.9 %iota_compare_fusion.5 = (pred[192]{0:T(512)(128)(4,1)}, pred[192]{0:T(512)(128)(4,1)}) fusion(s32[]{:T(128)} %bitcast.317, s32[]{:T(128)} %bitcast.314), kind=kLoop, calls=%fused_computation.524 | loop fusion | flops 384 | bytes 392 | tf_op jit(solution)/shard_map/lt | solution.py:32
  47.5 0.6 fusion.356
  48.4 0.3 fusion.279
  48.7 11.2 %all-to-all-done.1 = bf16[8,1,2,128,512]{4,3,2,1,0:T(8,128)(2,1)S(1)} async-done(((bf16[8,1,2,128,512]{4,3,2,1,0:T(8,128)(2,1)}), bf16[8,1,2,128,512]{4,3,2,1,0:T(8,128)(2,1)S(1)}, u32[]{:S(2)}, u32[]{:S(2)}) %all-to-all-start.1) | async-done | bytes 2097184 | tf_op jit(solution)/shard_map/all_to_all | solution.py:98
  59.8 0.2 copy.37
  60.1 0.2 fusion.380
  60.3 0.4 copy-done.8
  60.9 0.2 fusion.265
  61.6 0.2 fusion.269
  61.8 0.2 fusion.270
  62.0 0.2 fusion.271
  62.1 14.3 %conditional.8 = (bf16[5,4,1,2,128,128]{4,5,3,1,2,0:T(8,128)(2,1)}) conditional(s32[]{:T(128)} %convert_element_type.674, () %tuple.58, (bf16[1,2,128,512]{3,2,1,0:T(8,128)(2,1)S(1)}, s32[4]{0:T(128)S(1)}, bf16[1,256,192]{2,1,0:T(8,128)(2,1)S(1)}, s32[4]{0:T(128)S(1)}, bf16[1,256,192]{2,1,0:T(8,128)(2,1)S(1)}, ...), branch_computations={%region_1.2_spmd, %region_2.3_spmd} | conditional | flops 102236168 | bytes 6685032 | solution.py:112
  62.2 0.7 fusion.364
  64.7 0.2 convolution_bitcast_fusion.2
  67.6 0.2 convolution_bitcast_fusion.1
  70.5 0.2 convolution_bitcast_fusion
  73.3 0.2 convolution_bitcast_fusion.3
  74.3 1.4 %broadcast_in_dim.57 = bf16[5,4,1,2,128,128]{4,5,3,1,2,0:T(8,128)(2,1)} broadcast(bf16[]{:T(256)} %constant.228.clone), dimensions={} | broadcast | bytes 1310722 | tf_op jit(solution)/shard_map/broadcast_in_dim | solution.py:95
  75.7 0.7 fusion
  76.4 12.6 %conditional.9 = (bf16[5,4,1,2,128,128]{4,5,3,1,2,0:T(8,128)(2,1)}) conditional(s32[]{:T(128)} %convert_element_type.673, bf16[5,4,1,2,128,128]{4,5,3,1,2,0:T(8,128)(2,1)} %get-tuple-element.544, (bf16[1,2,128,512]{3,2,1,0:T(8,128)(2,1)S(1)}, s32[4]{0:T(128)S(1)}, bf16[1,256,192]{2,1,0:T(8,128)(2,1)S(1)}, s32[4]{0:T(128)S(1)}, ...), branch_computations={%region_3.4_spmd, %region_4.5_spmd} | conditional | flops 102236168 | bytes 5374310 | solution.py:112
  76.4 0.7 fusion.366
  78.9 0.2 convolution_bitcast_fusion.7
  81.7 0.2 convolution_bitcast_fusion.6
  84.6 0.2 convolution_bitcast_fusion.5
  87.2 0.2 convolution_bitcast_fusion.4
  88.2 0.7 fusion.33
  89.0 12.6 %conditional.10 = (bf16[5,4,1,2,128,128]{4,5,3,1,2,0:T(8,128)(2,1)}) conditional(s32[]{:T(128)} %convert_element_type.672, bf16[5,4,1,2,128,128]{4,5,3,1,2,0:T(8,128)(2,1)} %get-tuple-element.545, (bf16[1,2,128,512]{3,2,1,0:T(8,128)(2,1)S(1)}, s32[4]{0:T(128)S(1)}, bf16[1,256,192]{2,1,0:T(8,128)(2,1)S(1)}, s32[4]{0:T(128)S(1)}, ...), branch_computations={%region_5.6_spmd, %region_6.7_spmd} | conditional | flops 102236168 | bytes 5374310 | solution.py:112
  89.0 0.7 fusion.368
  91.5 0.2 convolution_bitcast_fusion.11
  94.3 0.2 convolution_bitcast_fusion.10
  97.2 0.2 convolution_bitcast_fusion.9
  99.8 0.2 convolution_bitcast_fusion.8
  100.8 0.7 fusion.66
  101.5 12.6 %conditional.11 = (bf16[5,4,1,2,128,128]{4,5,3,1,2,0:T(8,128)(2,1)}) conditional(s32[]{:T(128)} %convert_element_type.671, bf16[5,4,1,2,128,128]{4,5,3,1,2,0:T(8,128)(2,1)} %get-tuple-element.546, (bf16[1,2,128,512]{3,2,1,0:T(8,128)(2,1)S(1)}, s32[4]{0:T(128)S(1)}, bf16[1,256,192]{2,1,0:T(8,128)(2,1)S(1)}, s32[4]{0:T(128)S(1)}, ...), branch_computations={%region_7.8_spmd, %region_8.9_spmd} | conditional | flops 102236168 | bytes 5374310 | solution.py:112
  101.5 0.7 fusion.370
  104.0 0.2 convolution_bitcast_fusion.15
  106.9 0.2 convolution_bitcast_fusion.14
  109.7 0.2 convolution_bitcast_fusion.13
  112.4 0.2 convolution_bitcast_fusion.12
  113.3 0.7 fusion.99
  114.1 12.6 %conditional.12 = (bf16[5,4,1,2,128,128]{4,5,3,1,2,0:T(8,128)(2,1)}) conditional(s32[]{:T(128)} %convert_element_type.670, bf16[5,4,1,2,128,128]{4,5,3,1,2,0:T(8,128)(2,1)} %get-tuple-element.547, (bf16[1,2,128,512]{3,2,1,0:T(8,128)(2,1)S(1)}, s32[4]{0:T(128)S(1)}, bf16[1,256,192]{2,1,0:T(8,128)(2,1)S(1)}, s32[4]{0:T(128)S(1)}, ...), branch_computations={%region_9.10_spmd, %region_10.11_spmd} | conditional | flops 102236168 | bytes 5374310 | solution.py:112
  114.1 0.7 fusion.372
  116.6 0.2 convolution_bitcast_fusion.19
  119.4 0.2 convolution_bitcast_fusion.18
  122.3 0.2 convolution_bitcast_fusion.17
  124.9 0.2 convolution_bitcast_fusion.16
  125.9 0.7 fusion.132
  126.7 0.5 copy-done.15
  127.3 0.8 convolution_divide_fusion
  128.1 1.8 %conditional.15 = (bf16[1,5,4,1,2,128,128]{6,5,4,3,2,1,0:T(8,128)(2,1)S(1)}) conditional(s32[]{:T(128)} %convert_element_type.667, bf16[5,4,1,2,128,128]{4,5,3,1,0,2:T(8,128)(2,1)} %bitcast.324, (bf16[5,4,1,2,128,128]{4,5,3,1,2,0:T(8,128)(2,1)}, bf16[1,2,128,512]{3,2,1,0:T(8,128)(2,1)S(1)}, s32[4]{0:T(128)S(1)}, ...), branch_computations={%region_15.16_spmd, %region_16.17_spmd} | conditional | flops 102236168 | bytes 7995750 | solution.py:112
  128.1 1.8 %copy.43 = bf16[1,5,4,1,2,128,128]{6,5,4,3,2,1,0:T(8,128)(2,1)S(1)} copy(bf16[1,5,4,1,2,128,128]{5,6,4,2,3,1,0:T(8,128)(2,1)} %bitcast.266) | data formatting | bytes 2621440 | tf_op jit(solution)/shard_map/cond
  129.9 1.0 copy-done
  (85 shorter events, 1.9 us)
Async XLA Ops:
  27.1 6.5 %copy-start.2 = (s32[4]{0:T(128)S(1)}, s32[4]{0:T(128)}, u32[]{:S(2)}) copy-start(s32[4]{0:T(128)} %param.22) | copy-start | bytes 52
  27.1 20.2 %copy-start.1 = (bf16[2,256,1024]{2,1,0:T(8,128)(2,1)S(1)}, bf16[2,256,1024]{2,1,0:T(8,128)(2,1)}, u32[]{:S(2)}) copy-start(bf16[2,256,1024]{2,1,0:T(8,128)(2,1)} %param.23) | copy-start | bytes 3145732
  27.1 32.7 %all-to-all-start.1 = ((bf16[8,1,2,128,512]{4,3,2,1,0:T(8,128)(2,1)}), bf16[8,1,2,128,512]{4,3,2,1,0:T(8,128)(2,1)S(1)}, u32[]{:S(2)}, u32[]{:S(2)}) async-start(bf16[8,1,2,128,512]{4,3,2,1,0:T(8,128)(2,1)} %stack.365), calls=%async_computation.1 | async-start | bytes 4194304 | tf_op jit(solution)/shard_map/all_to_all | solution.py:98
  33.8 13.6 %copy-start.14 = (s32[4,1]{0,1:T(1,128)}, s32[4,1]{0,1:T(1,128)S(1)}, u32[]{:S(2)}) copy-start(s32[4,1]{0,1:T(1,128)S(1)} %reduce-window.8) | copy-start | bytes 52
  47.5 0.9 copy-start.10
  47.5 0.9 copy-start.11
  47.5 0.9 copy-start.12
  47.5 0.9 copy-start.13
  60.0 0.7 copy-start.8
  60.1 0.7 copy-start.9
  60.1 0.9 copy-start.6
  60.1 0.9 copy-start.7
  60.1 1.0 copy-start.4
  60.1 1.0 copy-start.5
  60.1 1.2 copy-start.3
  126.6 0.6 copy-start.15
  126.6 0.7 copy-start.16
  129.9 1.1 copy-start
